TPU v7x, 256 devices: a whole 4x4x8 slice. The times are simulated.
256 devices in a mesh: wall: 16 (over y, x_lo, core), span: 16 (over x_hi, z).
Axes of the slice: x: 4 (x_hi: 2, x_lo: 2; x = x_hi * 2 + x_lo), y: 4, z: 8, core: 2. Of those that a mesh axis runs over, the one named last changes fastest.
Arguments:
- field: float32 [4, 3, 2, 512, 6144], P(None, None, None, 'wall', 'span'), may hold values from -6 to 6
- mean_flow: float32 [2, 512], P(None, 'wall'), may hold values from 0.2 to 1.5
- d2_coef: float32 [15, 512], P(None, 'wall'), may hold values from -2 to 2
- wall_coef: float32 [2, 8], replicated, may hold values from -0.4375 to 0.4375
- kx_index: int32 [4], replicated, may hold values from 1 to 7
- patch_of: int32 [6144], P('span'), may hold values from 0 to 63
Outputs:
- new_field: float32 [4, 3, 2, 512, 6144], P(None, None, None, 'wall', 'span')
- wall_grad: float32 [2, 4, 2, 64], replicated
All inputs are finite; a program needn't handle non-finite values.
Results may differ from a plain program's by a relative error of at most 0.000073.
Values sent between devices are 32-bit elements; how exact they have to be, the bound alone decides.
A program may use at most 128 MiB of HBM per device.

v0:
```python
import math
import jax
import jax.numpy as jnp
from jax import lax
from jax.sharding import PartitionSpec as P

HALO = 7
STEN = 15
PATCH = 64
TAU = 0.25
VIS = 0.5


def with_halo(block, sides, width):
    for axis, dim in sides:
        count = lax.axis_size(axis)
        forward = [(i, i + 1) for i in range(count - 1)]
        backward = [(target, source) for source, target in forward]
        low = lax.ppermute(
            lax.slice_in_dim(block, block.shape[dim] - width, None, axis=dim), axis, forward
        )
        high = lax.ppermute(lax.slice_in_dim(block, 0, width, axis=dim), axis, backward)
        block = jnp.concatenate([low, block, high], axis=dim)
    return block


def spanwise_operator(line_data):
    item_count, part_count, row_count, length = line_data.shape
    inner_size = 128
    outer_size = length // inner_size
    highest = lax.Precision.HIGHEST
    real_part = line_data[:, 0].reshape(item_count, row_count, outer_size, inner_size)
    imag_part = line_data[:, 1].reshape(item_count, row_count, outer_size, inner_size)
    outer = jnp.arange(outer_size, dtype=jnp.int32)
    inner = jnp.arange(inner_size, dtype=jnp.int32)
    angle_one = (
        -2.0
        * math.pi
        / outer_size
        * (outer[:, None] * outer[None, :] % outer_size).astype(jnp.float32)
    )
    angle_two = (
        -2.0
        * math.pi
        / inner_size
        * (inner[:, None] * inner[None, :] % inner_size).astype(jnp.float32)
    )
    angle_twist = (
        -2.0 * math.pi / length * (outer[:, None] * inner[None, :] % length).astype(jnp.float32)
    )
    cos_one, sin_one = (jnp.cos(angle_one), jnp.sin(angle_one))
    cos_two, sin_two = (jnp.cos(angle_two), jnp.sin(angle_two))
    cos_twist, sin_twist = (jnp.cos(angle_twist), jnp.sin(angle_twist))

    def first_section(table, values):
        return jnp.einsum("kn,irnm->irkm", table, values, precision=highest)

    def second_section(values, table):
        return jnp.einsum("irkn,nm->irkm", values, table, precision=highest)

    def second_back(values, table):
        return jnp.einsum("irkm,nm->irkn", values, table, precision=highest)

    def first_back(table, values):
        return jnp.einsum("kn,irkm->irnm", table, values, precision=highest)

    section_real = first_section(cos_one, real_part) - first_section(sin_one, imag_part)
    section_imag = first_section(cos_one, imag_part) + first_section(sin_one, real_part)
    twist_real = section_real * cos_twist - section_imag * sin_twist
    twist_imag = section_real * sin_twist + section_imag * cos_twist
    modes_real = second_section(twist_real, cos_two) - second_section(twist_imag, sin_two)
    modes_imag = second_section(twist_real, sin_two) + second_section(twist_imag, cos_two)
    wave_index = outer[:, None] + outer_size * inner[None, :]
    signed = jnp.where(wave_index > length // 2, wave_index - length, wave_index)
    cutoff = length // 3
    wave_ratio = signed.astype(jnp.float32) / cutoff
    multiplier = jnp.where(
        jnp.abs(signed) < cutoff, -VIS * wave_ratio * wave_ratio, 0.0 * wave_ratio
    )
    modes_real = modes_real * multiplier
    modes_imag = modes_imag * multiplier
    back_real = second_back(modes_real, cos_two) + second_back(modes_imag, sin_two)
    back_imag = second_back(modes_imag, cos_two) - second_back(modes_real, sin_two)
    untwist_real = back_real * cos_twist + back_imag * sin_twist
    untwist_imag = back_imag * cos_twist - back_real * sin_twist
    result_real = (first_back(cos_one, untwist_real) + first_back(sin_one, untwist_imag)) / length
    result_imag = (first_back(cos_one, untwist_imag) - first_back(sin_one, untwist_real)) / length
    result_real = result_real.reshape(item_count, row_count, length)
    result_imag = result_imag.reshape(item_count, row_count, length)
    return jnp.stack([result_real, result_imag], axis=1)


def on_device(field, mean_flow, d2_coef, wall_coef, kx_index, patch_of):
    mode_count, comp_count, part_count, row_count, col_count = field.shape
    padded = with_halo(field, (("wall", 3),), HALO)
    diffusion = jnp.zeros_like(field)
    for offset in range(STEN):
        diffusion = (
            diffusion + d2_coef[offset][:, None] * padded[:, :, :, offset : offset + row_count, :]
        )
    flattened = field.reshape(mode_count * comp_count, part_count, row_count, col_count)
    spectral_lines = spanwise_operator(
        lax.all_to_all(flattened, "span", split_axis=2, concat_axis=3, tiled=True)
    )
    spanwise = lax.all_to_all(spectral_lines, "span", split_axis=3, concat_axis=2, tiled=True)
    spanwise = spanwise.reshape(field.shape)
    wave_number = kx_index.astype(jnp.float32) * 0.25
    velocity = mean_flow[0]
    shear_rate = mean_flow[1]
    advect_rate = wave_number[:, None, None, None] * velocity[None, None, :, None]
    advect_real = -advect_rate * field[:, :, 1]
    advect_imag = advect_rate * field[:, :, 0]
    advection = jnp.stack([advect_real, advect_imag], axis=2)
    coupling = shear_rate[None, None, :, None] * field[:, 0]
    advection = advection.at[:, 1].add(-coupling)
    new_field = field + TAU * advection + diffusion + spanwise
    lower_wall = jnp.zeros_like(new_field[:, 0, :, 0, :])
    upper_wall = jnp.zeros_like(new_field[:, 0, :, 0, :])
    for offset in range(HALO + 1):
        lower_wall = lower_wall + wall_coef[0, offset] * new_field[:, 0, :, offset, :]
        upper_wall = (
            upper_wall + wall_coef[1, offset] * new_field[:, 0, :, row_count - 1 - offset, :]
        )
    wall_index = lax.axis_index("wall")
    wall_count = lax.axis_size("wall")
    lower_wall = jnp.where(wall_index == 0, lower_wall, 0.0 * lower_wall)
    upper_wall = jnp.where(wall_index == wall_count - 1, upper_wall, 0.0 * upper_wall)
    shear_rows = jnp.stack([lower_wall, upper_wall])
    onehot = (patch_of[:, None] == jnp.arange(PATCH, dtype=jnp.int32)[None, :]).astype(jnp.float32)
    partial_grad = jnp.einsum("wmcz,zp->wmcp", shear_rows, onehot, precision=lax.Precision.HIGHEST)
    wall_grad = lax.psum(partial_grad, ("wall", "span"))
    return (new_field, wall_grad)


def solution(mesh):
    return jax.shard_map(
        on_device,
        mesh=mesh,
        in_specs=(
            P(None, None, None, "wall", "span"),
            P(None, "wall"),
            P(None, "wall"),
            P(),
            P(),
            P("span"),
        ),
        out_specs=(P(None, None, None, "wall", "span"), P()),
        check_vma=False,
    )
```

profile of v0, /device:TPU:1, one launch (start us, length us, event | category | flops | bytes accessed | tf_op | source)
XLA Modules:
  0.0 284.4 jit_solution(1954556570748203936)
XLA Ops:
  0.6 3.2 %copy.115 = f32[4,3,2,32,384]{4,2,1,0,3:T(2,128)} copy(f32[4,3,2,32,384]{4,3,2,1,0:T(8,128)} %param.8) | data formatting | bytes 2359296 | tf_op args[0]
  3.8 11.7 %all-to-all-start = ((f32[12,2,32,384]{3,1,0,2:T(2,128)}), f32[12,2,32,384]{3,1,0,2:T(2,128)S(1)}, u32[]{:S(2)}, u32[]{:S(2)}) async-start(f32[12,2,32,384]{3,1,0,2:T(2,128)} %bitcast.18), calls=%async_computation | async-start | bytes 2359296 | tf_op jit(solution)/shard_map/all_to_all | solution.py:103
  15.6 0.8 copy.109
  16.3 0.9 fusion.198
  17.2 3.0 %collective-permute-start = (f32[4,3,2,7,384]{4,0,2,3,1:T(4,128)}, f32[4,3,2,7,384]{4,0,2,3,1:T(4,128)}, u32[]{:S(2)}, u32[]{:S(2)}) collective-permute-start(f32[4,3,2,7,384]{4,0,2,3,1:T(4,128)} %get-tuple-element.32), channel_id=1, source_target_pairs={{0,16},{16,32},{32,48},{48,64},{64,80},{80,96},{96,112},{112,128},... | collective-permute-start | bytes 774152 | tf_op jit(solution)/shard_map/ppermute | solution.py:19
  20.3 2.0 collective-permute-start.1
  22.3 0.7 fusion.83
  23.0 0.6 multiply_select_fusion
  23.6 21.4 %all-to-all-done = f32[12,2,32,384]{3,1,0,2:T(2,128)S(1)} async-done(((f32[12,2,32,384]{3,1,0,2:T(2,128)}), f32[12,2,32,384]{3,1,0,2:T(2,128)S(1)}, u32[]{:S(2)}, u32[]{:S(2)}) %all-to-all-start) | async-done | bytes 1179680 | tf_op jit(solution)/shard_map/all_to_all | solution.py:103
  45.0 1.4 copy.116
  46.4 2.1 all_to_all.27
  49.1 0.8 fusion.77
  50.4 0.8 fusion.79
  51.1 0.8 convolution_add_fusion.3
  51.9 0.8 convolution_subtract_fusion.3
  52.7 0.9 fusion.24
  53.6 0.9 fusion.26
  54.5 0.9 fusion.4
  55.4 0.9 fusion.40
  56.3 0.9 fusion.5
  57.2 0.9 fusion.43
  58.0 0.9 convolution_subtract_fusion.1
  58.9 0.9 convolution_add_fusion.1
  59.8 0.8 fusion.32
  60.6 1.0 fusion.33
  61.7 0.8 fusion.3
  62.5 4.5 %copy.141 = f32[12,2,48,128]{0,1,3,2:T(2,128)} copy(f32[12,2,48,128]{3,2,1,0:T(8,128)S(1)} %fusion.3) | data formatting | bytes 1179648 | tf_op jit(solution)/shard_map/stack;reshape | solution.py:90
  67.0 1.6 fusion.1
  68.6 4.6 %copy.142 = f32[12,2,48,128]{0,1,3,2:T(2,128)} copy(f32[12,2,48,128]{3,2,1,0:T(8,128)S(1)} %fusion.1) | data formatting | bytes 1179648 | tf_op jit(solution)/shard_map/stack;reshape | solution.py:90
  73.2 11.8 %fusion.200 = f32[6144,2,2,12]{3,2,1,0:T(2,128)} fusion(f32[12,1,2,6144]{0,2,1,3:T(2,128)} %bitcast.155, f32[12,1,2,6144]{0,2,1,3:T(2,128)} %bitcast.154), kind=kLoop, calls=%fused_computation.261 | loop fusion | flops 294912 | bytes 2359296
  85.0 22.7 %reshape.465 = f32[16,1,18432]{2,1,0:T(1,128)} reshape(f32[6144,2,2,12]{3,2,1,0:T(2,128)} %fusion.200) | data formatting | bytes 2359296
  107.7 6.6 %all-to-all-start.1 = ((f32[16,1,18432]{2,1,0:T(1,128)}), f32[16,1,18432]{2,1,0:T(1,128)}, u32[]{:S(2)}, u32[]{:S(2)}) async-start(f32[16,1,18432]{2,1,0:T(1,128)} %reshape.465), calls=%async_computation.1 | async-start | bytes 2359296 | tf_op jit(solution)/shard_map/all_to_all | solution.py:105
  116.5 0.7 fusion.199
  117.3 1.0 fusion.30
  118.3 1.0 copy-done.3
  119.3 1.0 constant_dynamic-update-slice_fusion.1
  120.2 1.0 constant_dynamic-update-slice_fusion
  121.3 1.0 constant_dynamic-update-slice_fusion.2
  122.3 21.7 %all-to-all-done.1 = f32[16,1,18432]{2,1,0:T(1,128)} async-done(((f32[16,1,18432]{2,1,0:T(1,128)}), f32[16,1,18432]{2,1,0:T(1,128)}, u32[]{:S(2)}, u32[]{:S(2)}) %all-to-all-start.1) | async-done | bytes 1179680 | tf_op jit(solution)/shard_map/all_to_all | solution.py:105
  144.5 5.7 %reduce.2 = f32[16,18432]{1,0:T(8,128)} reduce(f32[16,1,18432]{2,1,0:T(1,128)} %all-to-all-done.1, f32[]{:T(128)} %broadcast.394), dimensions={1}, to_apply=%all_to_all.28.reduce_sub_computation | reduce | bytes 2359300 | tf_op jit(solution)/shard_map/all_to_all | solution.py:105
  150.2 27.5 %reshape.466 = f32[6144,2,2,12]{3,2,1,0:T(2,128)} reshape(f32[16,18432]{1,0:T(8,128)} %reduce.2) | data formatting | bytes 2359296
  177.7 11.2 %copy.143 = f32[12,2,2,16,384]{4,3,2,1,0:T(8,128)} copy(f32[12,2,2,16,384]{0,2,1,4,3:T(2,128)} %bitcast.153) | data formatting | bytes 2359296 | tf_op jit(solution)/shard_map/all_to_all | solution.py:105
  188.9 2.3 copy.124
  191.4 4.5 %fusion.8 = f32[4,3,2,32,384]{4,0,2,3,1:T(4,128)S(1)} fusion(f32[4,3,2,39,384]{4,0,2,3,1:T(4,128)S(1)} %constant_dynamic-update-slice_fusion.2, f32[4,3,2,39,384]{4,0,2,3,1:T(4,128)S(1)} %get-tuple-element.30, f32[4,3,2,32,384]{4,2,3,1,0:T(2,128)S(1)} %bitcast.156, f32[4,3,2,32,384]{4,0,2,3,1:T(4,128)S(1)} %copy-done.4, f32[32]{0:T(128)S(1)} %copy-done.19, ...), kind=kLoop, calls=%fused_computation.21 | loop fusion | flops 9732096 | bytes 21235584 | tf_op jit(solution)/shard_map/add | solution.py:116
  195.9 1.2 copy.126
  197.1 5.2 %multiply_select_fusion.1 = f32[1,4,2,384]{3,1,2,0:T(4,128)S(1)} fusion(f32[4,3,2,32,384]{4,0,2,3,1:T(4,128)S(1)} %fusion.8, f32[]{:T(128)} %bitcast.61, f32[]{:T(128)} %bitcast.60, f32[]{:T(128)} %bitcast.59, f32[]{:T(128)} %bitcast.58, f32[]{:T(128)} %bitcast.57, f32[]{:T(128)} %bitcast.56, f32[]{:T(128)} %bitcast.55, f32[]{:T(128)} %bitcast.54, pred[]{:T(512)S(6)} %eq.26), kind=kLoop, calls=%fused_computation.126 | loop fusion | flops 52224 | bytes 110625 | tf_op jit(solution)/shard_map/jit(_where)/select_n | solution.py:127
  202.4 5.1 %multiply_select_fusion.2 = f32[1,4,2,384]{3,1,2,0:T(4,128)S(1)} fusion(f32[4,3,2,32,384]{4,0,2,3,1:T(4,128)S(1)} %fusion.8, f32[]{:T(128)} %bitcast.52, f32[]{:T(128)} %bitcast.51, f32[]{:T(128)} %bitcast.50, f32[]{:T(128)} %bitcast.49, f32[]{:T(128)} %bitcast.48, f32[]{:T(128)} %bitcast.47, f32[]{:T(128)} %bitcast.46, f32[]{:T(128)} %bitcast.45, pred[]{:T(512)S(6)} %eq.25), kind=kLoop, calls=%fused_computation.127 | loop fusion | flops 52224 | bytes 110625 | tf_op jit(solution)/shard_map/jit(_where)/select_n | solution.py:126
  207.7 76.1 %psum.7 = f32[2,4,2,64]{3,1,2,0:T(4,128)S(1)} all-reduce(f32[2,4,2,64]{3,1,2,0:T(4,128)S(1)} %fusion.35), channel_id=1, replica_groups=mesh['wall'=16,'span'=16] {'wall','span'}, use_global_device_ids=true, to_apply=%region_0.1 | all-reduce | flops 1024 | bytes 8192 | tf_op jit(solution)/shard_map/psum | solution.py:131
  (62 shorter events, 4.6 us)
Async XLA Ops:
  3.8 11.7 %copy-start = (f32[4,3,2,32,384]{4,3,2,1,0:T(8,128)S(1)}, f32[4,3,2,32,384]{4,3,2,1,0:T(8,128)}, u32[]{:S(2)}) copy-start(f32[4,3,2,32,384]{4,3,2,1,0:T(8,128)} %param.8) | copy-start | bytes 3538948
  3.8 41.2 %all-to-all-start = ((f32[12,2,32,384]{3,1,0,2:T(2,128)}), f32[12,2,32,384]{3,1,0,2:T(2,128)S(1)}, u32[]{:S(2)}, u32[]{:S(2)}) async-start(f32[12,2,32,384]{3,1,0,2:T(2,128)} %bitcast.18), calls=%async_computation | async-start | bytes 2359296 | tf_op jit(solution)/shard_map/all_to_all | solution.py:103
  17.2 101.0 %collective-permute-start = (f32[4,3,2,7,384]{4,0,2,3,1:T(4,128)}, f32[4,3,2,7,384]{4,0,2,3,1:T(4,128)}, u32[]{:S(2)}, u32[]{:S(2)}) collective-permute-start(f32[4,3,2,7,384]{4,0,2,3,1:T(4,128)} %get-tuple-element.32), channel_id=1, source_target_pairs={{0,16},{16,32},{32,48},{48,64},{64,80},{80,96},{96,112},{112,128},... | collective-permute-start | bytes 774152 | tf_op jit(solution)/shard_map/ppermute | solution.py:19
  20.3 101.0 %collective-permute-start.1 = (f32[4,3,2,7,384]{4,0,2,3,1:T(4,128)}, f32[4,3,2,7,384]{4,0,2,3,1:T(4,128)}, u32[]{:S(2)}, u32[]{:S(2)}) collective-permute-start(f32[4,3,2,7,384]{4,0,2,3,1:T(4,128)} %get-tuple-element.33), channel_id=1, source_target_pairs={{16,0},{32,16},{48,32},{64,48},{80,64},{96,80},{112,96},{128,112},... | collective-permute-start | bytes 774152 | tf_op jit(solution)/shard_map/ppermute | solution.py:22
  51.9 0.8 copy-start.5
  51.9 0.8 copy-start.6
  53.6 0.9 copy-start.7
  107.7 6.7 %copy-start.23 = (s32[4]{0:T(128)S(1)}, s32[4]{0:T(128)}, u32[]{:S(2)}) copy-start(s32[4]{0:T(128)} %param.12) | copy-start | bytes 52
  107.7 6.7 %copy-start.21 = (f32[2,32]{1,0:T(2,128)S(1)}, f32[2,32]{1,0:T(2,128)}, u32[]{:S(2)}) copy-start(f32[2,32]{1,0:T(2,128)} %param.9) | copy-start | bytes 772
  107.7 36.3 %all-to-all-start.1 = ((f32[16,1,18432]{2,1,0:T(1,128)}), f32[16,1,18432]{2,1,0:T(1,128)}, u32[]{:S(2)}, u32[]{:S(2)}) async-start(f32[16,1,18432]{2,1,0:T(1,128)} %reshape.465), calls=%async_computation.1 | async-start | bytes 2359296 | tf_op jit(solution)/shard_map/all_to_all | solution.py:105
  115.2 0.7 copy-start.9
  115.2 1.3 copy-start.8
  117.3 3.0 %copy-start.1 = (f32[4,3,2,32,384]{4,3,2,1,0:T(8,128)S(1)}, f32[4,3,2,32,384]{4,3,2,1,0:T(8,128)}, u32[]{:S(2)}) copy-start(f32[4,3,2,32,384]{4,3,2,1,0:T(8,128)} %param.8) | copy-start | bytes 3538948
  118.2 1.0 copy-start.3
  188.8 2.4 copy-start.2
  188.8 2.4 copy-start.4
  188.8 2.5 copy-start.10
  188.8 2.5 copy-start.11
  188.9 2.5 copy-start.12
  188.9 2.5 copy-start.13
  188.9 2.5 copy-start.14
  188.9 2.5 copy-start.15
  188.9 2.5 copy-start.16
  188.9 2.5 copy-start.17
  188.9 2.5 copy-start.18
  188.9 2.5 copy-start.19
  188.9 2.5 copy-start.20
  195.9 11.6 %copy-start.22 = (s32[384]{0:T(512)S(1)}, s32[384]{0:T(512)}, u32[]{:S(2)}) copy-start(s32[384]{0:T(512)} %param.13) | copy-start | bytes 4612
where the time goes:
time: 286 us; the launch traced here: 284 us
  local copies, waits for them, and re-layouts  90.8 us (32%)
  blocking collectives  76.1 us (27%)
  waiting for transfers between devices  43.1 us (15%)
  other arithmetic  35.3 us (12%)
  starting transfers between devices  23.4 us (8%)
  matrix products  14.5 us (5%)
    psum x1, blocking collectives, on_device(): wall_grad = lax.psum(partial_grad, ('wall', 'span'))  76.1 us
    unnamed x55, local copies, waits for them, and re-layouts  58.4 us
    all_to_all x1, waiting for transfers between devices, on_device(): lax.all_to_all(spectral_lines, 'span', split_axis=3, concat_axis=2, tiled...  21.7 us
    all_to_all x1, waiting for transfers between devices, on_device(): lax.all_to_all(flattened, 'span', split_axis=2, concat_axis=3, tiled=True)  21.4 us
    all_to_all x3, local copies, waits for them, and re-layouts, on_device(): lax.all_to_all(spectral_lines, 'span', split_axis=3, concat_axis=2, tiled...  14 us
    unnamed x1, other arithmetic  11.8 us
    all_to_all x1, starting transfers between devices, on_device(): lax.all_to_all(flattened, 'span', split_axis=2, concat_axis=3, tiled=True)  11.7 us
    another operation x2, local copies, waits for them, and re-layouts, spanwise_operator(): return jnp.stack([result_real, result_imag], axis=1)  9.1 us
  transfers between devices with their start and end apart: 4, of which 2 were waited for; matrix products, arithmetic and copies ran while one was open for 25% of the time, Pallas kernels for 0%

commit v1 on v0

--- a/solution.py
+++ b/solution.py
@@ -128,7 +128,7 @@
     shear_rows = jnp.stack([lower_wall, upper_wall])
     onehot = (patch_of[:, None] == jnp.arange(PATCH, dtype=jnp.int32)[None, :]).astype(jnp.float32)
     partial_grad = jnp.einsum("wmcz,zp->wmcp", shear_rows, onehot, precision=lax.Precision.HIGHEST)
-    wall_grad = lax.psum(partial_grad, ("wall", "span"))
+    wall_grad = lax.psum(lax.psum(partial_grad, "wall"), "span")
     return (new_field, wall_grad)
 
 

time: 286 us -> 277 us (0.969)
  the two profiles are of different devices: /device:TPU:1 before, /device:TPU:4 now
where the time goes in v1:
time: 277 us; the launch traced here: 275 us
  local copies, waits for them, and re-layouts  90.9 us (33%)
  blocking collectives  68.4 us (25%)
  waiting for transfers between devices  42.9 us (15%)
  other arithmetic  35.2 us (13%)
  starting transfers between devices  22.3 us (8%)
  matrix products  14.5 us (5%)
    psum x2, blocking collectives, on_device(): wall_grad = lax.psum(lax.psum(partial_grad, 'wall'), 'span')  68.4 us
    unnamed x55, local copies, waits for them, and re-layouts  58.5 us
    all_to_all x1, waiting for transfers between devices, on_device(): lax.all_to_all(flattened, 'span', split_axis=2, concat_axis=3, tiled=True)  22.1 us
    all_to_all x1, waiting for transfers between devices, on_device(): lax.all_to_all(spectral_lines, 'span', split_axis=3, concat_axis=2, tiled...  20.8 us
    all_to_all x3, local copies, waits for them, and re-layouts, on_device(): lax.all_to_all(spectral_lines, 'span', split_axis=3, concat_axis=2, tiled...  14 us
    unnamed x1, other arithmetic  11.8 us
    all_to_all x1, starting transfers between devices, on_device(): lax.all_to_all(flattened, 'span', split_axis=2, concat_axis=3, tiled=True)  11.6 us
    another operation x2, local copies, waits for them, and re-layouts, spanwise_operator(): return jnp.stack([result_real, result_imag], axis=1)  9.11 us
  transfers between devices with their start and end apart: 4, of which 2 were waited for; matrix products, arithmetic and copies ran while one was open for 25% of the time, Pallas kernels for 0%

profile of v1, /device:TPU:4, one launch (start us, length us, event | category | flops | bytes accessed | tf_op | source)
XLA Modules:
  0.0 275.4 jit_solution(792947561176193262)
XLA Ops:
  0.6 3.2 %copy.115 = f32[4,3,2,32,384]{4,2,1,0,3:T(2,128)} copy(f32[4,3,2,32,384]{4,3,2,1,0:T(8,128)} %param.8) | data formatting | bytes 2359296 | tf_op args[0]
  3.8 11.6 %all-to-all-start = ((f32[12,2,32,384]{3,1,0,2:T(2,128)}), f32[12,2,32,384]{3,1,0,2:T(2,128)S(1)}, u32[]{:S(2)}, u32[]{:S(2)}) async-start(f32[12,2,32,384]{3,1,0,2:T(2,128)} %bitcast.18), calls=%async_computation | async-start | bytes 2359296 | tf_op jit(solution)/shard_map/all_to_all | solution.py:103
  15.4 0.8 copy.109
  16.2 0.9 fusion.198
  17.1 2.0 collective-permute-start
  19.1 1.3 collective-permute-start.1
  20.4 0.7 fusion.83
  21.8 22.1 %all-to-all-done = f32[12,2,32,384]{3,1,0,2:T(2,128)S(1)} async-done(((f32[12,2,32,384]{3,1,0,2:T(2,128)}), f32[12,2,32,384]{3,1,0,2:T(2,128)S(1)}, u32[]{:S(2)}, u32[]{:S(2)}) %all-to-all-start) | async-done | bytes 1179680 | tf_op jit(solution)/shard_map/all_to_all | solution.py:103
  43.9 1.4 copy.116
  45.3 2.1 all_to_all.27
  47.9 0.8 fusion.77
  49.2 0.8 fusion.79
  50.0 0.8 convolution_add_fusion.3
  50.8 0.8 convolution_subtract_fusion.3
  51.6 0.9 fusion.24
  52.5 0.9 fusion.26
  53.4 0.9 fusion.4
  54.2 0.9 fusion.40
  55.1 0.9 fusion.5
  56.0 0.9 fusion.43
  56.9 0.9 convolution_subtract_fusion.1
  57.8 0.9 convolution_add_fusion.1
  58.6 0.8 fusion.32
  59.5 1.0 fusion.33
  60.5 0.8 fusion.3
  61.4 4.5 %copy.141 = f32[12,2,48,128]{0,1,3,2:T(2,128)} copy(f32[12,2,48,128]{3,2,1,0:T(8,128)S(1)} %fusion.3) | data formatting | bytes 1179648 | tf_op jit(solution)/shard_map/stack;reshape | solution.py:90
  65.9 1.6 fusion.1
  67.5 4.6 %copy.142 = f32[12,2,48,128]{0,1,3,2:T(2,128)} copy(f32[12,2,48,128]{3,2,1,0:T(8,128)S(1)} %fusion.1) | data formatting | bytes 1179648 | tf_op jit(solution)/shard_map/stack;reshape | solution.py:90
  72.1 11.8 %fusion.200 = f32[6144,2,2,12]{3,2,1,0:T(2,128)} fusion(f32[12,1,2,6144]{0,2,1,3:T(2,128)} %bitcast.155, f32[12,1,2,6144]{0,2,1,3:T(2,128)} %bitcast.154), kind=kLoop, calls=%fused_computation.261 | loop fusion | flops 294912 | bytes 2359296
  83.8 22.7 %reshape.465 = f32[16,1,18432]{2,1,0:T(1,128)} reshape(f32[6144,2,2,12]{3,2,1,0:T(2,128)} %fusion.200) | data formatting | bytes 2359296
  106.5 7.4 %all-to-all-start.1 = ((f32[16,1,18432]{2,1,0:T(1,128)}), f32[16,1,18432]{2,1,0:T(1,128)}, u32[]{:S(2)}, u32[]{:S(2)}) async-start(f32[16,1,18432]{2,1,0:T(1,128)} %reshape.465), calls=%async_computation.1 | async-start | bytes 2359296 | tf_op jit(solution)/shard_map/all_to_all | solution.py:105
  116.2 0.7 fusion.199
  116.9 1.0 fusion.30
  117.9 1.0 copy-done.3
  119.0 1.0 constant_dynamic-update-slice_fusion.1
  119.9 1.0 constant_dynamic-update-slice_fusion
  121.0 1.0 constant_dynamic-update-slice_fusion.2
  122.0 20.8 %all-to-all-done.1 = f32[16,1,18432]{2,1,0:T(1,128)} async-done(((f32[16,1,18432]{2,1,0:T(1,128)}), f32[16,1,18432]{2,1,0:T(1,128)}, u32[]{:S(2)}, u32[]{:S(2)}) %all-to-all-start.1) | async-done | bytes 1179680 | tf_op jit(solution)/shard_map/all_to_all | solution.py:105
  143.3 5.7 %reduce.2 = f32[16,18432]{1,0:T(8,128)} reduce(f32[16,1,18432]{2,1,0:T(1,128)} %all-to-all-done.1, f32[]{:T(128)} %broadcast.394), dimensions={1}, to_apply=%all_to_all.28.reduce_sub_computation | reduce | bytes 2359300 | tf_op jit(solution)/shard_map/all_to_all | solution.py:105
  149.0 27.5 %reshape.466 = f32[6144,2,2,12]{3,2,1,0:T(2,128)} reshape(f32[16,18432]{1,0:T(8,128)} %reduce.2) | data formatting | bytes 2359296
  176.5 11.2 %copy.143 = f32[12,2,2,16,384]{4,3,2,1,0:T(8,128)} copy(f32[12,2,2,16,384]{0,2,1,4,3:T(2,128)} %bitcast.153) | data formatting | bytes 2359296 | tf_op jit(solution)/shard_map/all_to_all | solution.py:105
  187.7 2.3 copy.124
  190.2 4.5 %fusion.8 = f32[4,3,2,32,384]{4,0,2,3,1:T(4,128)S(1)} fusion(f32[4,3,2,39,384]{4,0,2,3,1:T(4,128)S(1)} %constant_dynamic-update-slice_fusion.2, f32[4,3,2,39,384]{4,0,2,3,1:T(4,128)S(1)} %get-tuple-element.30, f32[4,3,2,32,384]{4,2,3,1,0:T(2,128)S(1)} %bitcast.156, f32[4,3,2,32,384]{4,0,2,3,1:T(4,128)S(1)} %copy-done.4, f32[32]{0:T(128)S(1)} %copy-done.19, ...), kind=kLoop, calls=%fused_computation.21 | loop fusion | flops 9732096 | bytes 21235584 | tf_op jit(solution)/shard_map/add | solution.py:116
  194.7 1.2 copy.126
  195.9 5.2 %multiply_select_fusion.1 = f32[1,4,2,384]{3,1,2,0:T(4,128)S(1)} fusion(f32[4,3,2,32,384]{4,0,2,3,1:T(4,128)S(1)} %fusion.8, f32[]{:T(128)} %bitcast.61, f32[]{:T(128)} %bitcast.60, f32[]{:T(128)} %bitcast.59, f32[]{:T(128)} %bitcast.58, f32[]{:T(128)} %bitcast.57, f32[]{:T(128)} %bitcast.56, f32[]{:T(128)} %bitcast.55, f32[]{:T(128)} %bitcast.54, pred[]{:T(512)S(6)} %eq.26), kind=kLoop, calls=%fused_computation.126 | loop fusion | flops 52224 | bytes 110625 | tf_op jit(solution)/shard_map/jit(_where)/select_n | solution.py:127
  201.1 5.0 %multiply_select_fusion.2 = f32[1,4,2,384]{3,1,2,0:T(4,128)S(1)} fusion(f32[4,3,2,32,384]{4,0,2,3,1:T(4,128)S(1)} %fusion.8, f32[]{:T(128)} %bitcast.52, f32[]{:T(128)} %bitcast.51, f32[]{:T(128)} %bitcast.50, f32[]{:T(128)} %bitcast.49, f32[]{:T(128)} %bitcast.48, f32[]{:T(128)} %bitcast.47, f32[]{:T(128)} %bitcast.46, f32[]{:T(128)} %bitcast.45, pred[]{:T(512)S(6)} %eq.25), kind=kLoop, calls=%fused_computation.127 | loop fusion | flops 52224 | bytes 110625 | tf_op jit(solution)/shard_map/jit(_where)/select_n | solution.py:126
  206.4 28.1 %psum.14 = f32[2,4,2,64]{3,1,2,0:T(4,128)S(1)} all-reduce(f32[2,4,2,64]{3,1,2,0:T(4,128)S(1)} %fusion.35), channel_id=1, replica_groups=mesh['wall'=16,'span'=16] {'wall'}, use_global_device_ids=true, to_apply=%region_0.1 | all-reduce | flops 1024 | bytes 8192 | tf_op jit(solution)/shard_map/psum | solution.py:131
  234.5 40.3 %psum.15 = f32[2,4,2,64]{3,1,2,0:T(4,128)S(1)} all-reduce(f32[2,4,2,64]{3,1,2,0:T(4,128)S(1)} %psum.14), channel_id=1, replica_groups=mesh['wall'=16,'span'=16] {'span'}, use_global_device_ids=true, to_apply=%region_1.2 | all-reduce | flops 1024 | bytes 8192 | tf_op jit(solution)/shard_map/psum | solution.py:131
  (63 shorter events, 5.2 us)
Async XLA Ops:
  3.8 11.6 %copy-start = (f32[4,3,2,32,384]{4,3,2,1,0:T(8,128)S(1)}, f32[4,3,2,32,384]{4,3,2,1,0:T(8,128)}, u32[]{:S(2)}) copy-start(f32[4,3,2,32,384]{4,3,2,1,0:T(8,128)} %param.8) | copy-start | bytes 3538948
  3.8 40.1 %all-to-all-start = ((f32[12,2,32,384]{3,1,0,2:T(2,128)}), f32[12,2,32,384]{3,1,0,2:T(2,128)S(1)}, u32[]{:S(2)}, u32[]{:S(2)}) async-start(f32[12,2,32,384]{3,1,0,2:T(2,128)} %bitcast.18), calls=%async_computation | async-start | bytes 2359296 | tf_op jit(solution)/shard_map/all_to_all | solution.py:103
  17.1 100.8 %collective-permute-start = (f32[4,3,2,7,384]{4,0,2,3,1:T(4,128)}, f32[4,3,2,7,384]{4,0,2,3,1:T(4,128)}, u32[]{:S(2)}, u32[]{:S(2)}) collective-permute-start(f32[4,3,2,7,384]{4,0,2,3,1:T(4,128)} %get-tuple-element.32), channel_id=1, source_target_pairs={{0,16},{16,32},{32,48},{48,64},{64,80},{80,96},{96,112},{112,128},... | collective-permute-start | bytes 774152 | tf_op jit(solution)/shard_map/ppermute | solution.py:19
  19.1 101.9 %collective-permute-start.1 = (f32[4,3,2,7,384]{4,0,2,3,1:T(4,128)}, f32[4,3,2,7,384]{4,0,2,3,1:T(4,128)}, u32[]{:S(2)}, u32[]{:S(2)}) collective-permute-start(f32[4,3,2,7,384]{4,0,2,3,1:T(4,128)} %get-tuple-element.33), channel_id=1, source_target_pairs={{16,0},{32,16},{48,32},{64,48},{80,64},{96,80},{112,96},{128,112},... | collective-permute-start | bytes 774152 | tf_op jit(solution)/shard_map/ppermute | solution.py:22
  50.8 0.8 copy-start.5
  50.8 0.8 copy-start.6
  52.5 0.9 copy-start.7
  106.5 7.5 %copy-start.23 = (s32[4]{0:T(128)S(1)}, s32[4]{0:T(128)}, u32[]{:S(2)}) copy-start(s32[4]{0:T(128)} %param.12) | copy-start | bytes 52
  106.5 7.5 %copy-start.21 = (f32[2,32]{1,0:T(2,128)S(1)}, f32[2,32]{1,0:T(2,128)}, u32[]{:S(2)}) copy-start(f32[2,32]{1,0:T(2,128)} %param.9) | copy-start | bytes 772
  106.5 36.2 %all-to-all-start.1 = ((f32[16,1,18432]{2,1,0:T(1,128)}), f32[16,1,18432]{2,1,0:T(1,128)}, u32[]{:S(2)}, u32[]{:S(2)}) async-start(f32[16,1,18432]{2,1,0:T(1,128)} %reshape.465), calls=%async_computation.1 | async-start | bytes 2359296 | tf_op jit(solution)/shard_map/all_to_all | solution.py:105
  114.9 0.7 copy-start.9
  114.9 1.3 copy-start.8
  116.9 3.0 %copy-start.1 = (f32[4,3,2,32,384]{4,3,2,1,0:T(8,128)S(1)}, f32[4,3,2,32,384]{4,3,2,1,0:T(8,128)}, u32[]{:S(2)}) copy-start(f32[4,3,2,32,384]{4,3,2,1,0:T(8,128)} %param.8) | copy-start | bytes 3538948
  117.9 1.0 copy-start.3
  187.6 2.4 copy-start.2
  187.6 2.4 copy-start.4
  187.6 2.5 copy-start.10
  187.6 2.5 copy-start.11
  187.6 2.5 copy-start.12
  187.6 2.5 copy-start.13
  187.7 2.5 copy-start.14
  187.7 2.5 copy-start.15
  187.7 2.5 copy-start.16
  187.7 2.5 copy-start.17
  187.7 2.5 copy-start.18
  187.7 2.5 copy-start.19
  187.7 2.5 copy-start.20
  194.7 11.5 %copy-start.22 = (s32[384]{0:T(512)S(1)}, s32[384]{0:T(512)}, u32[]{:S(2)}) copy-start(s32[384]{0:T(512)} %param.13) | copy-start | bytes 4612
